TPU v7x, 128 devices: a whole 4x4x4 slice. The times are simulated.
128 devices in a mesh: gx: 4 (over y), gy: 32 (over z, x, core).
Axes of the slice: x: 4, y: 4, z: 4, core: 2. Of those that a mesh axis runs over, the one named last changes fastest.
Arguments:
- labels: float32 [524288, 256], P(('gx', 'gy')), may hold values from 0 to 24, as said below
- weights: bfloat16 [4096, 12, 128, 128], P(('gx', 'gy')), may hold values from 0.001 to 1, as said below
- column_index: int32 [4096, 12], P(('gx', 'gy')), may hold values from 0 to 47, as said below
- send_index: int32 [128, 4, 4], P(('gx', 'gy')), may hold values from 0 to 31, as said below
- seed_doc: int32 [32768], P(('gx', 'gy')), may hold values from 0 to 4095
- seed_topic: int32 [32768], P(('gx', 'gy')), may hold values from 0 to 255
Outputs:
- spread: float32 [524288, 256], P(('gx', 'gy'))
Inputs may be any that keep to these rules, and one draw needn't show every extreme that they name: `column_index`: slot 0 of a row block names the row block itself (its index within the partition). A value below 32 names a block of the partition's own labels; 32 + d * 4 + s names slot s of what neighbour d hands over; only existing neighbours are named, and only in the last 3 slots. `send_index`: the 4 entries of one partition and direction are distinct. `weights`: entries are positive. `labels`: entries are nonnegative.
All inputs are finite; a program needn't handle non-finite values.
Results may differ from a plain program's by a relative error of at most 0.0004.
Values may be sent and summed in bfloat16 or wider, within the bound.
A program may use at most 128 MiB of HBM per device.

v0:
```python
import jax
import jax.numpy as jnp
from jax import lax
from jax.sharding import PartitionSpec as P

ITERS = 2


ALPHA = 0.99
GAIN = 1.0 / (1.0 - 0.99)


def shifted(value, axis, steps):
    count = lax.axis_size(axis)
    initial, last = (max(0, -steps), min(count, count - steps))
    return lax.ppermute(value, axis, [(source, source + steps) for source in range(initial, last)])


def local(labels, weights, column_index, send_index, seed_doc, seed_topic):
    blocks_dev, slots, block_size, _ = weights.shape
    documents = blocks_dev * block_size
    topics = labels.shape[1]
    ones_vector = jnp.ones((block_size,), jnp.bfloat16)
    degree = jnp.einsum("rkij,j->ri", weights, ones_vector, preferred_element_type=jnp.float32)
    scale = (1.0 / jnp.sqrt(degree)).reshape(documents, 1)
    doc_hot = (seed_doc[:, None] == jnp.arange(documents, dtype=jnp.int32)[None, :]).astype(
        jnp.bfloat16
    )
    topic_hot = (seed_topic[:, None] == jnp.arange(topics, dtype=jnp.int32)[None, :]).astype(
        jnp.bfloat16
    )
    counts = lax.dot_general(
        doc_hot, topic_hot, (((0,), (0,)), ((), ())), preferred_element_type=jnp.float32
    )
    seeds = counts * GAIN
    seed_term = (1.0 - ALPHA) * seeds
    lists = send_index[0]
    current = labels
    for iteration in range(ITERS):
        scaled = (scale * current).astype(jnp.bfloat16).reshape(blocks_dev, block_size, topics)
        outgoing = scaled[lists]
        lower_inner = shifted(outgoing[1], "gy", 1)
        upper_inner = shifted(outgoing[0], "gy", -1)
        lower_outer = shifted(outgoing[3], "gx", 1)
        upper_outer = shifted(outgoing[2], "gx", -1)
        extended = jnp.concatenate(
            [scaled, lower_inner, upper_inner, lower_outer, upper_outer], axis=0
        )
        picked = extended[column_index]
        product = jnp.einsum("rkij,rkjc->ric", weights, picked, preferred_element_type=jnp.float32)
        current = ALPHA * scale * product.reshape(documents, topics) + seed_term
    return current


def solution(mesh):
    in_specs = (
        P(("gx", "gy"), None),
        P(("gx", "gy"), None, None, None),
        P(("gx", "gy"), None),
        P(("gx", "gy"), None, None),
        P(("gx", "gy")),
        P(("gx", "gy")),
    )
    out_specs = P(("gx", "gy"), None)
    return jax.shard_map(local, mesh=mesh, in_specs=in_specs, out_specs=out_specs, check_vma=False)
```

profile of v0, /device:TPU:104, one launch (start us, length us, event | category | flops | bytes accessed | tf_op | source)
XLA Modules:
  0.0 126.2 jit_solution(2295635474505666051)
XLA Ops:
  0.0 0.7 compare_select_fusion.1
  0.7 0.1 reshape.60
  0.8 7.4 %convert_reduce_fusion = bf16[32,128,128]{2,1,0:T(8,128)(2,1)S(1)} fusion(bf16[32,12,128,128]{3,2,1,0:T(8,128)(2,1)} %param.7), kind=kLoop, calls=%fused_computation.4 | loop fusion | flops 12058624 | bytes 13631488 | tf_op jit(solution)/shard_map/rkij,j->ri/reduce_sum | solution.py:24
  8.2 0.4 fusion.7
  8.5 0.0 copy-start.2
  8.6 2.6 %multiply_convert_fusion = bf16[4096,256]{1,0:T(8,128)(2,1)S(1)} fusion(f32[4096,256]{1,0:T(8,128)} %param.6, f32[4096]{0:T(1024)S(1)} %rsqrt_bitcast_fusion), kind=kLoop, calls=%fused_computation.12 | loop fusion | flops 2097152 | bytes 6307840 | tf_op jit(solution)/shard_map/convert_element_type | solution.py:40
  11.2 0.0 copy-start
  11.2 0.6 gather_fusion
  11.8 1.0 fusion.11
  12.8 2.3 %collective-permute-start.3 = (bf16[4,128,256]{2,1,0:T(8,128)(2,1)}, bf16[4,128,256]{2,1,0:T(8,128)(2,1)S(1)}, u32[]{:S(2)}, u32[]{:S(2)}) collective-permute-start(bf16[4,128,256]{2,1,0:T(8,128)(2,1)} %get-tuple-element.9), channel_id=1, source_target_pairs={{32,0},{64,32},{96,64},{33,1},{65,33},{97,65},{34,2},{66,34},{98,6... | collective-permute-start | bytes 786440 | tf_op jit(solution)/shard_map/ppermute | solution.py:16
  15.2 3.5 %collective-permute-start.2 = (bf16[4,128,256]{2,1,0:T(8,128)(2,1)}, bf16[4,128,256]{2,1,0:T(8,128)(2,1)}, u32[]{:S(2)}, u32[]{:S(2)}) collective-permute-start(bf16[4,128,256]{2,1,0:T(8,128)(2,1)} %get-tuple-element.10), channel_id=1, source_target_pairs={{0,32},{32,64},{64,96},{1,33},{33,65},{65,97},{2,34},{34,66},{66,9... | collective-permute-start | bytes 786440 | tf_op jit(solution)/shard_map/ppermute | solution.py:16
  18.7 3.4 %collective-permute-start.1 = (bf16[4,128,256]{2,1,0:T(8,128)(2,1)}, bf16[4,128,256]{2,1,0:T(8,128)(2,1)}, u32[]{:S(2)}, u32[]{:S(2)}) collective-permute-start(bf16[4,128,256]{2,1,0:T(8,128)(2,1)} %get-tuple-element.11), channel_id=1, source_target_pairs={{1,0},{2,1},{3,2},{4,3},{5,4},{6,5},{7,6},{8,7},{9,8},{10,9},{11,1... | collective-permute-start | bytes 786440 | tf_op jit(solution)/shard_map/ppermute | solution.py:16
  22.1 1.9 %collective-permute-start = (bf16[4,128,256]{2,1,0:T(8,128)(2,1)}, bf16[4,128,256]{2,1,0:T(8,128)(2,1)}, u32[]{:S(2)}, u32[]{:S(2)}) collective-permute-start(bf16[4,128,256]{2,1,0:T(8,128)(2,1)} %get-tuple-element.12), channel_id=1, source_target_pairs={{0,1},{1,2},{2,3},{3,4},{4,5},{5,6},{6,7},{7,8},{8,9},{9,10},{10,1... | collective-permute-start | bytes 786440 | tf_op jit(solution)/shard_map/ppermute | solution.py:16
  24.0 0.0 copy-done
  24.0 0.0 copy-done.2
  24.1 1.7 %constant_dynamic-update-slice_fusion.4 = bf16[48,128,256]{2,1,0:T(8,128)(2,1)S(1)} fusion(bf16[32,128,256]{2,1,0:T(8,128)(2,1)} %bitcast.44), kind=kLoop, calls=%fused_computation.22 | loop fusion | bytes 4194304
  25.8 0.1 copy.7
  25.9 0.1 reshape.68
  26.0 6.2 %collective-permute-done = bf16[4,128,256]{2,1,0:T(8,128)(2,1)} collective-permute-done((bf16[4,128,256]{2,1,0:T(8,128)(2,1)}, bf16[4,128,256]{2,1,0:T(8,128)(2,1)}, u32[]{:S(2)}, u32[]{:S(2)}) %collective-permute-start) | collective-permute-done | bytes 262176 | tf_op jit(solution)/shard_map/ppermute | solution.py:16
  32.2 1.0 constant_dynamic-update-slice_fusion.3
  33.2 0.0 collective-permute-done.1
  33.2 1.0 constant_dynamic-update-slice_fusion.2
  34.2 0.0 collective-permute-done.2
  34.2 1.0 constant_dynamic-update-slice_fusion.1
  35.1 0.0 collective-permute-done.3
  35.2 12.9 %gather_fusion.1 = bf16[384,128,256]{2,1,0:T(8,128)(2,1)} fusion(bf16[48,128,256]{2,1,0:T(8,128)(2,1)S(1)} %constant_dynamic-update-slice_fusion, s32[1024]{0:T(1024)S(1)} %pad_clamp_fusion), kind=kCustom, calls=%fused_computation.1 | custom fusion | bytes 50333184 | tf_op jit(solution)/shard_map/gather | solution.py:49
  48.1 0.0 copy-start.3
  48.1 0.0 copy-start.4
  48.1 16.5 %fusion.12 = f32[32,256,128,1]{1,2,3,0:T(8,128)} fusion(bf16[32,12,128,128]{3,2,1,0:T(8,128)(2,1)} %param.7, bf16[32,12,128,256]{3,2,1,0:T(8,128)(2,1)} %bitcast.42), kind=kOutput, calls=%fused_computation.38 | convolution fusion | flops 3221225472 | bytes 41943040 | tf_op jit(solution)/shard_map/rkij,rkjc->ric/dot_general | solution.py:50
  64.6 0.0 copy-done.3
  64.6 0.0 copy-done.4
  64.6 5.4 %fusion.3 = (bf16[4096,256]{1,0:T(8,128)(2,1)S(1)}, f32[4096,256]{1,0:T(8,128)}) fusion(f32[32,256,128,1]{1,2,3,0:T(8,128)} %fusion.12, f32[4096]{0:T(1024)S(1)} %rsqrt_bitcast_fusion, f32[4096]{0:T(1024)S(1)} %broadcast_multiply_fusion, s32[256]{0:T(256)S(1)} %copy-done.3, s32[256]{0:T(256)S(1)} %copy-done.4), kind=kOutput, calls=%fused_computation.10 | convolution fusion | flops 542179328 | bytes 10520576 | tf_op jit(solution)/shard_map/dot_general | solution.py:32
  70.0 0.0 copy-start.1
  70.0 0.6 gather_fusion.2
  70.6 0.1 fusion.10
  70.7 1.9 %collective-permute-start.4 = (bf16[4,128,256]{2,1,0:T(8,128)(2,1)S(1)}, bf16[4,128,256]{2,1,0:T(8,128)(2,1)S(1)}, u32[]{:S(2)}, u32[]{:S(2)}) collective-permute-start(bf16[4,128,256]{2,1,0:T(8,128)(2,1)S(1)} %get-tuple-element.8), channel_id=1, source_target_pairs={{0,1},{1,2},{2,3},{3,4},{4,5},{5,6},{6,7},{7,8},{8,9},{9,10},{10,1... | collective-permute-start | bytes 786440 | tf_op jit(solution)/shard_map/ppermute | solution.py:16
  72.6 3.5 %collective-permute-start.6 = (bf16[4,128,256]{2,1,0:T(8,128)(2,1)S(1)}, bf16[4,128,256]{2,1,0:T(8,128)(2,1)S(1)}, u32[]{:S(2)}, u32[]{:S(2)}) collective-permute-start(bf16[4,128,256]{2,1,0:T(8,128)(2,1)S(1)} %get-tuple-element.6), channel_id=1, source_target_pairs={{0,32},{32,64},{64,96},{1,33},{33,65},{65,97},{2,34},{34,66},{66,9... | collective-permute-start | bytes 786440 | tf_op jit(solution)/shard_map/ppermute | solution.py:16
  76.2 0.0 copy-done.1
  76.2 5.5 %collective-permute-start.5 = (bf16[4,128,256]{2,1,0:T(8,128)(2,1)S(1)}, bf16[4,128,256]{2,1,0:T(8,128)(2,1)S(1)}, u32[]{:S(2)}, u32[]{:S(2)}) collective-permute-start(bf16[4,128,256]{2,1,0:T(8,128)(2,1)S(1)} %get-tuple-element.7), channel_id=1, source_target_pairs={{1,0},{2,1},{3,2},{4,3},{5,4},{6,5},{7,6},{8,7},{9,8},{10,9},{11,1... | collective-permute-start | bytes 786440 | tf_op jit(solution)/shard_map/ppermute | solution.py:16
  81.7 1.7 %constant_dynamic-update-slice_fusion.9 = bf16[48,128,256]{2,1,0:T(8,128)(2,1)S(1)} fusion(bf16[32,128,256]{2,1,0:T(8,128)(2,1)} %bitcast.46), kind=kLoop, calls=%fused_computation.27 | loop fusion | bytes 4194304
  83.4 2.5 %collective-permute-start.7 = (bf16[4,128,256]{2,1,0:T(8,128)(2,1)S(1)}, bf16[4,128,256]{2,1,0:T(8,128)(2,1)S(1)}, u32[]{:S(2)}, u32[]{:S(2)}) collective-permute-start(bf16[4,128,256]{2,1,0:T(8,128)(2,1)S(1)} %get-tuple-element.5), channel_id=1, source_target_pairs={{32,0},{64,32},{96,64},{33,1},{65,33},{97,65},{34,2},{66,34},{98,6... | collective-permute-start | bytes 786440 | tf_op jit(solution)/shard_map/ppermute | solution.py:16
  85.9 0.0 collective-permute-done.4
  85.9 0.0 collective-permute-done.5
  86.0 0.0 collective-permute-done.6
  86.0 5.6 %collective-permute-done.7 = bf16[4,128,256]{2,1,0:T(8,128)(2,1)S(1)} collective-permute-done((bf16[4,128,256]{2,1,0:T(8,128)(2,1)S(1)}, bf16[4,128,256]{2,1,0:T(8,128)(2,1)S(1)}, u32[]{:S(2)}, u32[]{:S(2)}) %collective-permute-start.7) | collective-permute-done | bytes 262176 | tf_op jit(solution)/shard_map/ppermute | solution.py:16
  91.7 12.9 %gather_fusion.3 = bf16[384,128,256]{2,1,0:T(8,128)(2,1)} fusion(bf16[48,128,256]{2,1,0:T(8,128)(2,1)S(1)} %constant_dynamic-update-slice_fusion.5, s32[1024]{0:T(1024)S(1)} %pad_clamp_fusion), kind=kCustom, calls=%fused_computation.3 | custom fusion | bytes 50333184 | tf_op jit(solution)/shard_map/gather | solution.py:49
  104.6 16.5 %fusion.13 = f32[32,256,128,1]{1,2,3,0:T(8,128)} fusion(bf16[32,12,128,128]{3,2,1,0:T(8,128)(2,1)} %param.7, bf16[32,12,128,256]{3,2,1,0:T(8,128)(2,1)} %bitcast.41), kind=kOutput, calls=%fused_computation.39 | convolution fusion | flops 3221225472 | bytes 41943040 | tf_op jit(solution)/shard_map/rkij,rkjc->ric/dot_general | solution.py:50
  121.1 5.1 %fusion = f32[4096,256]{1,0:T(8,128)} fusion(f32[4096,256]{1,0:T(8,128)} %get-tuple-element.14, f32[32,256,128,1]{1,2,3,0:T(8,128)} %fusion.13, f32[4096]{0:T(1024)S(1)} %broadcast_multiply_fusion), kind=kLoop, calls=%fused_computation.6 | loop fusion | flops 2097152 | bytes 12599296 | tf_op jit(solution)/shard_map/add | solution.py:51
  (10 shorter events, 0.1 us)
Async XLA Ops:
  8.5 15.5 %copy-start.2 = (s32[32,12]{0,1:T(8,128)S(1)}, s32[32,12]{0,1:T(8,128)}, u32[]{:S(2)}) copy-start(s32[32,12]{0,1:T(8,128)} %param.8) | copy-start | bytes 4612
  11.2 12.9 %copy-start = (bf16[4096,256]{1,0:T(8,128)(2,1)}, bf16[4096,256]{1,0:T(8,128)(2,1)S(1)}, u32[]{:S(2)}) copy-start(bf16[4096,256]{1,0:T(8,128)(2,1)S(1)} %multiply_convert_fusion) | copy-start | bytes 6291460
  12.8 22.3 %collective-permute-start.3 = (bf16[4,128,256]{2,1,0:T(8,128)(2,1)}, bf16[4,128,256]{2,1,0:T(8,128)(2,1)S(1)}, u32[]{:S(2)}, u32[]{:S(2)}) collective-permute-start(bf16[4,128,256]{2,1,0:T(8,128)(2,1)} %get-tuple-element.9), channel_id=1, source_target_pairs={{32,0},{64,32},{96,64},{33,1},{65,33},{97,65},{34,2},{66,34},{98,6... | collective-permute-start | bytes 786440 | tf_op jit(solution)/shard_map/ppermute | solution.py:16
  15.2 19.0 %collective-permute-start.2 = (bf16[4,128,256]{2,1,0:T(8,128)(2,1)}, bf16[4,128,256]{2,1,0:T(8,128)(2,1)}, u32[]{:S(2)}, u32[]{:S(2)}) collective-permute-start(bf16[4,128,256]{2,1,0:T(8,128)(2,1)} %get-tuple-element.10), channel_id=1, source_target_pairs={{0,32},{32,64},{64,96},{1,33},{33,65},{65,97},{2,34},{34,66},{66,9... | collective-permute-start | bytes 786440 | tf_op jit(solution)/shard_map/ppermute | solution.py:16
  18.7 14.5 %collective-permute-start.1 = (bf16[4,128,256]{2,1,0:T(8,128)(2,1)}, bf16[4,128,256]{2,1,0:T(8,128)(2,1)}, u32[]{:S(2)}, u32[]{:S(2)}) collective-permute-start(bf16[4,128,256]{2,1,0:T(8,128)(2,1)} %get-tuple-element.11), channel_id=1, source_target_pairs={{1,0},{2,1},{3,2},{4,3},{5,4},{6,5},{7,6},{8,7},{9,8},{10,9},{11,1... | collective-permute-start | bytes 786440 | tf_op jit(solution)/shard_map/ppermute | solution.py:16
  22.1 10.1 %collective-permute-start = (bf16[4,128,256]{2,1,0:T(8,128)(2,1)}, bf16[4,128,256]{2,1,0:T(8,128)(2,1)}, u32[]{:S(2)}, u32[]{:S(2)}) collective-permute-start(bf16[4,128,256]{2,1,0:T(8,128)(2,1)} %get-tuple-element.12), channel_id=1, source_target_pairs={{0,1},{1,2},{2,3},{3,4},{4,5},{5,6},{6,7},{7,8},{8,9},{9,10},{10,1... | collective-permute-start | bytes 786440 | tf_op jit(solution)/shard_map/ppermute | solution.py:16
  48.1 16.5 %copy-start.3 = (s32[256]{0:T(256)S(1)}, s32[256]{0:T(256)}, u32[]{:S(2)}) copy-start(s32[256]{0:T(256)} %param.11) | copy-start | bytes 3076
  48.1 16.5 %copy-start.4 = (s32[256]{0:T(256)S(1)}, s32[256]{0:T(256)}, u32[]{:S(2)}) copy-start(s32[256]{0:T(256)} %param.10) | copy-start | bytes 3076
  70.0 6.2 %copy-start.1 = (bf16[4096,256]{1,0:T(8,128)(2,1)}, bf16[4096,256]{1,0:T(8,128)(2,1)S(1)}, u32[]{:S(2)}) copy-start(bf16[4096,256]{1,0:T(8,128)(2,1)S(1)} %get-tuple-element.13) | copy-start | bytes 6291460
  70.7 15.2 %collective-permute-start.4 = (bf16[4,128,256]{2,1,0:T(8,128)(2,1)S(1)}, bf16[4,128,256]{2,1,0:T(8,128)(2,1)S(1)}, u32[]{:S(2)}, u32[]{:S(2)}) collective-permute-start(bf16[4,128,256]{2,1,0:T(8,128)(2,1)S(1)} %get-tuple-element.8), channel_id=1, source_target_pairs={{0,1},{1,2},{2,3},{3,4},{4,5},{5,6},{6,7},{7,8},{8,9},{9,10},{10,1... | collective-permute-start | bytes 786440 | tf_op jit(solution)/shard_map/ppermute | solution.py:16
  72.6 13.4 %collective-permute-start.6 = (bf16[4,128,256]{2,1,0:T(8,128)(2,1)S(1)}, bf16[4,128,256]{2,1,0:T(8,128)(2,1)S(1)}, u32[]{:S(2)}, u32[]{:S(2)}) collective-permute-start(bf16[4,128,256]{2,1,0:T(8,128)(2,1)S(1)} %get-tuple-element.6), channel_id=1, source_target_pairs={{0,32},{32,64},{64,96},{1,33},{33,65},{65,97},{2,34},{34,66},{66,9... | collective-permute-start | bytes 786440 | tf_op jit(solution)/shard_map/ppermute | solution.py:16
  76.2 9.8 %collective-permute-start.5 = (bf16[4,128,256]{2,1,0:T(8,128)(2,1)S(1)}, bf16[4,128,256]{2,1,0:T(8,128)(2,1)S(1)}, u32[]{:S(2)}, u32[]{:S(2)}) collective-permute-start(bf16[4,128,256]{2,1,0:T(8,128)(2,1)S(1)} %get-tuple-element.7), channel_id=1, source_target_pairs={{1,0},{2,1},{3,2},{4,3},{5,4},{6,5},{7,6},{8,7},{9,8},{10,9},{11,1... | collective-permute-start | bytes 786440 | tf_op jit(solution)/shard_map/ppermute | solution.py:16
  83.4 8.3 %collective-permute-start.7 = (bf16[4,128,256]{2,1,0:T(8,128)(2,1)S(1)}, bf16[4,128,256]{2,1,0:T(8,128)(2,1)S(1)}, u32[]{:S(2)}, u32[]{:S(2)}) collective-permute-start(bf16[4,128,256]{2,1,0:T(8,128)(2,1)S(1)} %get-tuple-element.5), channel_id=1, source_target_pairs={{32,0},{64,32},{96,64},{33,1},{65,33},{97,65},{34,2},{66,34},{98,6... | collective-permute-start | bytes 786440 | tf_op jit(solution)/shard_map/ppermute | solution.py:16
where the time goes:
time: 127 us; the launch traced here: 126 us
  matrix products  38.8 us (31%)
  local copies, waits for them, and re-layouts  34.9 us (27%)
  starting transfers between devices  24.6 us (19%)
  other arithmetic  15.8 us (12%)
  waiting for transfers between devices  11.9 us (9%)
    dot_general x2, matrix products, local(): jnp.einsum('rkij,rkjc->ric', weights, picked, preferred_element_type=jnp....  33 us
    gather x2, local copies, waits for them, and re-layouts, local(): picked = extended[column_index]  25.8 us
    ppermute x8, starting transfers between devices, shifted(): lax.ppermute(value, axis, [(source, source + steps) for source in range(i...  24.6 us
    ppermute x8, waiting for transfers between devices, shifted(): lax.ppermute(value, axis, [(source, source + steps) for source in range(i...  11.9 us
    reduce_sum x1, other arithmetic, local(): jnp.einsum('rkij,j->ri', weights, ones_vector, preferred_element_type=jnp...  7.38 us
    unnamed x18, local copies, waits for them, and re-layouts  6.45 us
    dot_general x1, matrix products, local(): lax.dot_general(doc_hot, topic_hot, (((0,), (0,)), ((), ())), preferred_e...  5.4 us
    add x1, other arithmetic, local(): current = ALPHA * scale * product.reshape(documents, topics) + seed_term  5.13 us
  transfers between devices with their start and end apart: 8, of which 2 were waited for; matrix products, arithmetic and copies ran while one was open for 5% of the time, Pallas kernels for 0%

commit v1 on v0

v1 whole, which is shorter than its diff:
```python
import functools

import jax
import jax.numpy as jnp
from jax import lax
from jax.experimental import pallas as pl
from jax.experimental.pallas import tpu as pltpu
from jax.sharding import PartitionSpec as P

ALPHA = 0.99
GAIN = 1.0 / (1.0 - 0.99)
SEED = (1.0 - ALPHA) * GAIN

MESH = pl.DeviceIdType.MESH
BF16 = jnp.bfloat16
F32 = jnp.float32
VMEM = pl.BlockSpec(memory_space=pltpu.VMEM)
SMEM = pl.BlockSpec(memory_space=pltpu.SMEM)
HBM = pl.BlockSpec(memory_space=pl.ANY)

EARLY = 8
CHUNK = 4
UNROLL = 8
DIRS = (2, 3, 0, 1)


def block_row(weight_ref, labels_ref, column_ref, row, first):
    count = weight_ref.shape[1]
    left = jnp.concatenate([weight_ref[row, k] for k in range(count)], axis=1)
    right = jnp.concatenate([labels_ref[column_ref[row, first + k]] for k in range(count)], axis=0)
    return jnp.dot(left, right, preferred_element_type=F32)


def doubled(scale):
    return jnp.concatenate([scale, scale], axis=1)


def spread_kernel(
    sizes,
    column_ref,
    send_ref,
    doc_ref,
    topic_ref,
    labels_hbm,
    weights_hbm,
    late_ref,
    next_ref,
    partial_ref,
    scale_ref,
    early_ref,
    labels_ref,
    now_ref,
    first_ref,
    count_ref,
    hot_ref,
    stage_a,
    stage_b,
    halo_a,
    halo_b,
    rows_out,
    rows_in,
    label_sem,
    early_sem,
    late_sem,
    send_a,
    recv_a,
    send_b,
    recv_b,
    send_s,
    recv_s,
):
    outer, inner = sizes
    blocks, block, topics = labels_hbm.shape
    sends = send_ref.shape[1]
    a, b = lax.axis_index("gx"), lax.axis_index("gy")
    has = [b > 0, b < inner - 1, a > 0, a < outer - 1]
    peer = [
        {"gx": a, "gy": b - 1},
        {"gx": a, "gy": b + 1},
        {"gx": a - 1, "gy": b},
        {"gx": a + 1, "gy": b},
    ]

    def remote(src, dst, send_sem, recv_sem, d):
        return pltpu.make_async_remote_copy(
            src_ref=src,
            dst_ref=dst,
            send_sem=send_sem,
            recv_sem=recv_sem,
            device_id=peer[d],
            device_id_type=MESH,
        )

    chunks = blocks // CHUNK
    label_copy = pltpu.make_async_copy(labels_hbm, labels_ref, label_sem)

    def early_copy(c):
        rows = pl.ds(c * CHUNK, CHUNK)
        return pltpu.make_async_copy(
            weights_hbm.at[rows, pl.ds(0, EARLY)], early_ref.at[rows], early_sem.at[c]
        )

    def late_copy(c):
        rows = pl.ds(c * CHUNK, CHUNK)
        late = weights_hbm.shape[1] - EARLY
        return pltpu.make_async_copy(
            weights_hbm.at[rows, pl.ds(EARLY, late)], late_ref.at[rows], late_sem.at[c]
        )

    label_copy.start()
    for c in range(2):
        early_copy(c).start()
        late_copy(c).start()

    barrier = pltpu.get_barrier_semaphore()
    for d in range(4):

        @pl.when(has[d])
        def _():
            pl.semaphore_signal(barrier, inc=1, device_id=peer[d], device_id_type=MESH)

    seeds = doc_ref.shape[1]
    wanted = jnp.broadcast_to(topic_ref[...], (topics, seeds))
    ours = lax.broadcasted_iota(jnp.int32, (topics, seeds), 0)
    hot_ref[...] = jnp.where(wanted == ours, 1.0, 0.0).astype(F32).T.astype(BF16)

    def count_rows(g, carry):
        for u in range(CHUNK):
            r = g * CHUNK + u
            docs = lax.broadcasted_iota(jnp.int32, (block, seeds), 0) + r * block
            hot = jnp.where(docs == jnp.broadcast_to(doc_ref[...], (block, seeds)), 1.0, 0.0)
            found = jnp.dot(hot.astype(BF16), hot_ref[...], preferred_element_type=F32)
            count_ref[r] = found.astype(BF16)
        return carry

    lax.fori_loop(0, chunks, count_rows, 0)

    pl.semaphore_wait(barrier, sum(jnp.where(h, 1, 0) for h in has))

    label_copy.wait()
    for c in range(2, chunks):
        early_copy(c).start()
        late_copy(c).start()
    for d in DIRS:
        for s in range(sends):
            stage_a[d, s] = labels_ref[send_ref[d, s]].astype(BF16)

        @pl.when(has[d])
        def _():
            remote(stage_a.at[d], halo_a.at[d ^ 1], send_a.at[d], recv_a.at[d ^ 1], d).start()

    def degree_rows(c, carry):
        early_copy(c).wait()
        late_copy(c).wait()
        for u in range(CHUNK):
            r = c * CHUNK + u
            total = early_ref[r, 0].astype(F32)
            for k in range(1, EARLY):
                total = total + early_ref[r, k].astype(F32)
            for k in range(late_ref.shape[1]):
                total = total + late_ref[r, k].astype(F32)
            degree = jnp.sum(total, axis=1, keepdims=True)
            scale = jnp.broadcast_to(1.0 / jnp.sqrt(degree), (block, block))
            scale_ref[r] = scale
            now_ref[r] = (doubled(scale) * labels_ref[r]).astype(BF16)
        return carry

    lax.fori_loop(0, chunks, degree_rows, 0)

    lanes = lax.broadcasted_iota(jnp.int32, (block, block), 1)
    columns = jnp.zeros((block, block), F32)
    for d in range(4):
        for s in range(sends):
            columns = jnp.where(lanes == d * 8 + s, scale_ref[send_ref[d, s]], columns)
    rows = columns.T
    for d in DIRS:
        rows_out[d] = rows[d * 8 : d * 8 + 8]

        @pl.when(has[d])
        def _():
            remote(rows_out.at[d], rows_in.at[d ^ 1], send_s.at[d], recv_s.at[d ^ 1], d).start()

    def first_early(g, carry):
        for u in range(UNROLL):
            r = g * UNROLL + u
            first_ref[r] = block_row(early_ref, now_ref, column_ref, r, 0)
        return carry

    lax.fori_loop(0, blocks // UNROLL, first_early, 0)

    for d in range(4):

        @pl.when(has[d])
        def _():
            remote(stage_a.at[d], halo_a.at[d], send_a.at[d], recv_a.at[d], d).wait_recv()
            remote(rows_out.at[d], rows_in.at[d], send_s.at[d], recv_s.at[d], d).wait_recv()

        @pl.when(jnp.logical_not(has[d]))
        def _():
            rows_in[d] = jnp.zeros(rows_in.shape[1:], F32)
            halo_a[d] = jnp.zeros(halo_a.shape[1:], BF16)

    taken = jnp.concatenate(
        [rows_in[d] for d in range(4)] + [jnp.zeros((block - 32, block), F32)], axis=0
    )
    scales = taken.T
    for d in range(4):
        for s in range(sends):
            scale = jnp.broadcast_to(scales[:, d * 8 + s : d * 8 + s + 1], (block, topics))
            now_ref[blocks + d * sends + s] = (scale * halo_a[d, s].astype(F32)).astype(BF16)

    def next_scaled(r):
        scale = doubled(scale_ref[r])
        product = first_ref[r] + block_row(late_ref, now_ref, column_ref, r, EARLY)
        current = ALPHA * scale * product + SEED * count_ref[r].astype(F32)
        return (scale * current).astype(BF16)

    def sent_rows(s, carry):
        for d in DIRS:
            stage_b[d, s] = next_scaled(send_ref[d, s])
        for d in DIRS:

            @pl.when(has[d])
            def _():
                remote(
                    stage_b.at[d, s], halo_b.at[d ^ 1, s], send_b.at[d, s], recv_b.at[d ^ 1, s], d
                ).start()

        return carry

    lax.fori_loop(0, sends, sent_rows, 0)

    def first_late(g, carry):
        for u in range(UNROLL):
            r = g * UNROLL + u
            next_ref[r] = next_scaled(r)
        return carry

    lax.fori_loop(0, blocks // UNROLL, first_late, 0)

    def second_early(g, carry):
        for u in range(UNROLL):
            r = g * UNROLL + u
            product = block_row(early_ref, next_ref, column_ref, r, 0)
            scale = doubled(scale_ref[r])
            partial_ref[r] = ALPHA * scale * product + SEED * count_ref[r].astype(F32)
        return carry

    lax.fori_loop(0, blocks // UNROLL, second_early, 0)

    for d in range(4):

        @pl.when(has[d])
        def _():
            for s in range(sends):
                remote(
                    stage_b.at[d, s], halo_b.at[d, s], send_b.at[d, s], recv_b.at[d, s], d
                ).wait_recv()

        @pl.when(jnp.logical_not(has[d]))
        def _():
            halo_b[d] = jnp.zeros(halo_b.shape[1:], BF16)

    for d in range(4):
        for s in range(sends):
            next_ref[blocks + d * sends + s] = halo_b[d, s]

    for d in range(4):

        @pl.when(has[d])
        def _():
            remote(stage_a.at[d], halo_a.at[d], send_a.at[d], recv_a.at[d], d).wait_send()
            remote(rows_out.at[d], rows_in.at[d], send_s.at[d], recv_s.at[d], d).wait_send()
            for s in range(sends):
                remote(
                    stage_b.at[d, s], halo_b.at[d, s], send_b.at[d, s], recv_b.at[d, s], d
                ).wait_send()


def finish_kernel(column_ref, late_ref, next_ref, partial_ref, scale_ref, out_ref):
    g = pl.program_id(0)
    for u in range(out_ref.shape[0]):
        r = g * out_ref.shape[0] + u
        product = block_row(late_ref, next_ref, column_ref, r, EARLY)
        out_ref[u] = partial_ref[r] + ALPHA * doubled(scale_ref[r]) * product


def local(sizes, labels, weights, column_index, send_index, seed_doc, seed_topic):
    blocks, slots, block, _ = weights.shape
    topics = labels.shape[1]
    dirs, sends = send_index.shape[1:]
    halo = dirs * sends
    chunks = blocks // CHUNK
    late, following, partial, scale = pl.pallas_call(
        functools.partial(spread_kernel, sizes),
        out_shape=(
            jax.ShapeDtypeStruct((blocks, slots - EARLY, block, block), BF16),
            jax.ShapeDtypeStruct((blocks + halo, block, topics), BF16),
            jax.ShapeDtypeStruct((blocks, block, topics), F32),
            jax.ShapeDtypeStruct((blocks, block, block), F32),
        ),
        in_specs=[SMEM, SMEM, VMEM, VMEM, HBM, HBM],
        out_specs=(VMEM, VMEM, VMEM, VMEM),
        scratch_shapes=[
            pltpu.VMEM((blocks, EARLY, block, block), BF16),
            pltpu.VMEM((blocks, block, topics), F32),
            pltpu.VMEM((blocks + halo, block, topics), BF16),
            pltpu.VMEM((blocks, block, topics), F32),
            pltpu.VMEM((blocks, block, topics), BF16),
            pltpu.VMEM((seed_doc.shape[0], topics), BF16),
            pltpu.VMEM((dirs, sends, block, topics), BF16),
            pltpu.VMEM((dirs, sends, block, topics), BF16),
            pltpu.VMEM((dirs, sends, block, topics), BF16),
            pltpu.VMEM((dirs, sends, block, topics), BF16),
            pltpu.VMEM((dirs, 8, block), F32),
            pltpu.VMEM((dirs, 8, block), F32),
            pltpu.SemaphoreType.DMA,
            pltpu.SemaphoreType.DMA((chunks,)),
            pltpu.SemaphoreType.DMA((chunks,)),
            pltpu.SemaphoreType.DMA((dirs,)),
            pltpu.SemaphoreType.DMA((dirs,)),
            pltpu.SemaphoreType.DMA((dirs, sends)),
            pltpu.SemaphoreType.DMA((dirs, sends)),
            pltpu.SemaphoreType.DMA((dirs,)),
            pltpu.SemaphoreType.DMA((dirs,)),
        ],
        compiler_params=pltpu.CompilerParams(
            collective_id=0, has_side_effects=True, vmem_limit_bytes=38 << 20
        ),
        name="spread",
    )(
        column_index,
        send_index.reshape(dirs, sends),
        seed_doc.reshape(1, -1),
        seed_topic.reshape(1, -1),
        labels.reshape(blocks, block, topics),
        weights,
    )
    out = pl.pallas_call(
        finish_kernel,
        grid=(blocks // UNROLL,),
        out_shape=jax.ShapeDtypeStruct((blocks, block, topics), F32),
        in_specs=[SMEM, VMEM, VMEM, VMEM, VMEM],
        out_specs=pl.BlockSpec((UNROLL, block, topics), lambda g: (g, 0, 0)),
        compiler_params=pltpu.CompilerParams(vmem_limit_bytes=30 << 20),
        name="finish",
    )(column_index, late, following, partial, scale)
    return out.reshape(blocks * block, topics)


def solution(mesh):
    sizes = (mesh.shape["gx"], mesh.shape["gy"])
    parts = P(("gx", "gy"))
    return jax.shard_map(
        functools.partial(local, sizes),
        mesh=mesh,
        in_specs=(parts,) * 6,
        out_specs=parts,
        check_vma=False,
    )
```

time: 127 us -> 27.8 us (0.22)
  matrix products: 38.8 us -> 0 us
  local copies, waits for them, and re-layouts: 34.9 us -> 2.81 us
  Pallas kernels: 0 us -> 24.7 us
  starting transfers between devices: 24.6 us -> 0 us
  other arithmetic: 15.8 us -> 0 us
  waiting for transfers between devices: 11.9 us -> 0 us
    dot_general x4 -> x0, matrix products: 38.8 us -> none  [the longest x2 33 us: local(): jnp.einsum('rkij,rkjc->ric', weights, picked, preferred_element_type=jnp....]
    gather x4 -> x0, local copies, waits for them, and re-layouts: 27 us -> none  [the longest x2 25.8 us: local(): picked = extended[column_index]]
    pallas_call x0 -> x2, Pallas kernels: none -> 24.7 us  [the longest x1 20.4 us: local(): pl.pallas_call(functools.partial(spread_kernel, sizes), out_shape=(jax.Sh...]
    ppermute x8 -> x0, starting transfers between devices: 24.6 us -> none  [shifted(): lax.ppermute(value, axis, [(source, source + steps) for source in range(i...]
    ppermute x8 -> x0, waiting for transfers between devices: 11.9 us -> none  [shifted(): lax.ppermute(value, axis, [(source, source + steps) for source in range(i...]
    reduce_sum x1 -> x0, other arithmetic: 7.38 us -> none  [local(): jnp.einsum('rkij,j->ri', weights, ones_vector, preferred_element_type=jnp...]
    add x1 -> x0, other arithmetic: 5.13 us -> none  [local(): current = ALPHA * scale * product.reshape(documents, topics) + seed_term]
    unnamed x18 -> x7, local copies, waits for them, and re-layouts: 6.45 us -> 2.81 us
  transfers between devices with their start and end apart: 8 -> 0, of which waited for: 2 -> 0; matrix products, arithmetic and copies ran while one was open for 5% -> 0% of each run, Pallas kernels for 0% -> 0%
where the time goes in v1:
time: 27.8 us; the launch traced here: 27.5 us
  Pallas kernels  24.7 us (89%)
  local copies, waits for them, and re-layouts  2.81 us (10%)
    pallas_call x1, Pallas kernels, local(): pl.pallas_call(functools.partial(spread_kernel, sizes), out_shape=(jax.Sh...  20.4 us
    pallas_call x1, Pallas kernels, local(): pl.pallas_call(finish_kernel, grid=(blocks // UNROLL,), out_shape=jax.Sha...  4.33 us
    unnamed x7, local copies, waits for them, and re-layouts  2.81 us

profile of v1, /device:TPU:104, one launch (start us, length us, event | category | flops | bytes accessed | tf_op | source)
XLA Modules:
  0.0 27.5 jit_solution(6283637217575813358)
XLA Ops:
  0.0 0.8 %copy.8.column_ref = s32[32,12]{1,0:T(8,128)S(1)} copy(s32[32,12]{0,1:T(8,128)} %param.8) | data formatting | bytes 3072 | tf_op args[2]
  0.8 0.0 copy-start
  0.8 0.7 %copy-done = s32[1,4,4]{2,1,0:T(4,128)S(1)} copy-done((s32[1,4,4]{2,1,0:T(4,128)S(1)}, s32[1,4,4]{2,1,0:T(4,128)}, u32[]{:S(2)}) %copy-start) | copy-done | bytes 88
  1.5 0.0 copy-start.1
  1.5 0.7 %copy-done.1 = s32[256]{0:T(256)S(1)} copy-done((s32[256]{0:T(256)S(1)}, s32[256]{0:T(256)}, u32[]{:S(2)}) %copy-start.1) | copy-done | bytes 1048
  2.1 0.0 copy-start.2
  2.1 0.7 %copy-done.2 = s32[256]{0:T(256)S(1)} copy-done((s32[256]{0:T(256)S(1)}, s32[256]{0:T(256)}, u32[]{:S(2)}) %copy-start.2) | copy-done | bytes 1048
  2.8 20.4 %spread.1 = (bf16[32,4,128,128]{3,2,1,0:T(8,128)(2,1)S(1)}, bf16[48,128,256]{2,1,0:T(8,128)(2,1)S(1)}, f32[32,128,256]{2,1,0:T(8,128)S(1)}, f32[32,128,128]{2,1,0:T(8,128)S(1)}) custom-call(s32[32,12]{1,0:T(8,128)S(1)} %copy.8.column_ref, s32[4,4]{1,0:T(4,128)S(1)} %bitcast.5, s32[1,256]{1,0:T(1,128)S(1)} %bitcast.6, s32[1,256]{1,0:T(1,128)S(1)} %bitcast.7, ...), custom_call_target="tpu_custom_call" | custom-call | tf_op jit(solution)/shard_map/spread/pallas_call | solution.py:294
  23.2 4.3 %finish.1 = f32[32,128,256]{2,1,0:T(8,128)} custom-call(s32[32,12]{1,0:T(8,128)S(1)} %copy.8.column_ref, bf16[32,4,128,128]{3,2,1,0:T(8,128)(2,1)S(1)} %get-tuple-element.9.late_ref, bf16[48,128,256]{2,1,0:T(8,128)(2,1)S(1)} %get-tuple-element.10.next_ref, f32[32,128,256]{2,1,0:T(8,128)S(1)} %get-tuple-element.11.partial_ref, ...), custom_call_target="tpu_custom_call" | custom-call | tf_op jit(solution)/shard_map/finish/pallas_call | solution.py:339
Async XLA Ops:
  0.8 0.7 %copy-start = (s32[1,4,4]{2,1,0:T(4,128)S(1)}, s32[1,4,4]{2,1,0:T(4,128)}, u32[]{:S(2)}) copy-start(s32[1,4,4]{2,1,0:T(4,128)} %param.9) | copy-start | bytes 196
  1.5 0.7 %copy-start.1 = (s32[256]{0:T(256)S(1)}, s32[256]{0:T(256)}, u32[]{:S(2)}) copy-start(s32[256]{0:T(256)} %param.10) | copy-start | bytes 3076
  2.1 0.7 %copy-start.2 = (s32[256]{0:T(256)S(1)}, s32[256]{0:T(256)}, u32[]{:S(2)}) copy-start(s32[256]{0:T(256)} %param.11) | copy-start | bytes 3076

commit v2 on v1

v2 whole, which is shorter than its diff:
```python
import functools

import jax
import jax.numpy as jnp
from jax import lax
from jax.experimental import pallas as pl
from jax.experimental.pallas import tpu as pltpu
from jax.sharding import PartitionSpec as P

ALPHA = 0.99
GAIN = 1.0 / (1.0 - 0.99)
SEED = (1.0 - ALPHA) * GAIN

MESH = pl.DeviceIdType.MESH
BF16 = jnp.bfloat16
F32 = jnp.float32
VMEM = pl.BlockSpec(memory_space=pltpu.VMEM)
HBM = pl.BlockSpec(memory_space=pl.ANY)

EARLY = 8
CHUNK = 4
FIRST = 1
WIDE = 16
GROUP = 4
DIRS = (2, 3, 0, 1)


def block_row(parts, labels_ref, table_ref, row):
    left, right = [], []
    for weight_ref, first in parts:
        for k in range(weight_ref.shape[1]):
            left.append(weight_ref[row, k])
            right.append(labels_ref[table_ref[first + k, row]])
    return jnp.dot(
        jnp.concatenate(left, axis=1),
        jnp.concatenate(right, axis=0),
        preferred_element_type=F32,
    )


def doubled(scale):
    return jnp.concatenate([scale, scale], axis=1)


def spread_kernel(
    sizes,
    whole_ref,
    labels_hbm,
    weights_hbm,
    late_ref,
    next_ref,
    partial_ref,
    scale_ref,
    table_ref,
    early_ref,
    labels_ref,
    now_ref,
    first_ref,
    count_ref,
    hot_ref,
    stage_a,
    stage_b,
    halo_a,
    mine_ref,
    rows_out,
    rows_in,
    table_sem,
    label_sem,
    early_sem,
    late_sem,
    send_a,
    recv_a,
    send_b,
    recv_b,
    send_s,
    recv_s,
):
    outer, inner = sizes
    blocks, block, topics = labels_hbm.shape
    seeds = whole_ref.shape[1]
    sends = halo_a.shape[1]
    slots = weights_hbm.shape[1]
    a, b = lax.axis_index("gx"), lax.axis_index("gy")
    has = [b > 0, b < inner - 1, a > 0, a < outer - 1]
    peer = [
        {"gx": a, "gy": b - 1},
        {"gx": a, "gy": b + 1},
        {"gx": a - 1, "gy": b},
        {"gx": a + 1, "gy": b},
    ]

    def remote(src, dst, send_sem, recv_sem, d):
        return pltpu.make_async_remote_copy(
            src_ref=src,
            dst_ref=dst,
            send_sem=send_sem,
            recv_sem=recv_sem,
            device_id=peer[d],
            device_id_type=MESH,
        )

    chunks = blocks // CHUNK
    label_copy = pltpu.make_async_copy(labels_hbm, labels_ref, label_sem)

    def early_copy(c):
        rows = pl.ds(c * CHUNK, CHUNK)
        return pltpu.make_async_copy(
            weights_hbm.at[rows, pl.ds(0, EARLY)], early_ref.at[rows], early_sem.at[c]
        )

    def late_copy(c):
        rows = pl.ds(c * CHUNK, CHUNK)
        late = weights_hbm.shape[1] - EARLY
        return pltpu.make_async_copy(
            weights_hbm.at[rows, pl.ds(EARLY, late)], late_ref.at[rows], late_sem.at[c]
        )

    label_copy.start()
    table_copy = pltpu.make_async_copy(whole_ref.at[0:16, 0:128], table_ref, table_sem)
    table_copy.start()
    for c in range(FIRST):
        early_copy(c).start()
        late_copy(c).start()

    barrier = pltpu.get_barrier_semaphore()
    for d in range(4):

        @pl.when(has[d])
        def _():
            pl.semaphore_signal(barrier, inc=1, device_id=peer[d], device_id_type=MESH)

    pl.semaphore_wait(barrier, sum(jnp.where(h, 1, 0) for h in has))

    table_copy.wait()
    label_copy.wait()
    for c in range(FIRST, chunks):
        early_copy(c).start()
        late_copy(c).start()
    for d in DIRS:
        for s in range(sends):
            stage_a[d, s] = labels_ref[table_ref[slots + d, s]].astype(BF16)

        @pl.when(has[d])
        def _():
            remote(stage_a.at[d], halo_a.at[d ^ 1], send_a.at[d], recv_a.at[d ^ 1], d).start()

    wanted = jnp.broadcast_to(whole_ref[17:18], (topics, seeds))
    ours = lax.broadcasted_iota(jnp.int32, (topics, seeds), 0)
    hot_ref[...] = jnp.where(wanted == ours, 1.0, 0.0).astype(F32).T.astype(BF16)

    wanted_docs = jnp.broadcast_to(whole_ref[16:17], (block, seeds))

    def count_rows(g, carry):
        for u in range(CHUNK):
            r = g * CHUNK + u
            docs = lax.broadcasted_iota(jnp.int32, (block, seeds), 0) + r * block
            hot = jnp.where(docs == wanted_docs, 1.0, 0.0)
            found = jnp.dot(hot.astype(BF16), hot_ref[...], preferred_element_type=F32)
            count_ref[r] = found.astype(BF16)
        return carry

    lax.fori_loop(0, chunks, count_rows, 0)

    def degree_rows(c, carry):
        early_copy(c).wait()
        late_copy(c).wait()
        for u in range(CHUNK):
            r = c * CHUNK + u
            total = early_ref[r, 0].astype(F32)
            for k in range(1, EARLY):
                total = total + early_ref[r, k].astype(F32)
            for k in range(late_ref.shape[1]):
                total = total + late_ref[r, k].astype(F32)
            degree = jnp.sum(total, axis=1, keepdims=True)
            scale = jnp.broadcast_to(1.0 / jnp.sqrt(degree), (block, block))
            scale_ref[r] = scale
            now_ref[r] = (doubled(scale) * labels_ref[r]).astype(BF16)
        return carry

    lax.fori_loop(0, chunks, degree_rows, 0)

    lanes = lax.broadcasted_iota(jnp.int32, (block, block), 1)
    columns = jnp.zeros((block, block), F32)
    for d in range(4):
        for s in range(sends):
            columns = jnp.where(lanes == d * 8 + s, scale_ref[table_ref[slots + d, s]], columns)
    rows = columns.T
    for d in DIRS:
        rows_out[d] = rows[d * 8 : d * 8 + 8]

        @pl.when(has[d])
        def _():
            remote(rows_out.at[d], rows_in.at[d ^ 1], send_s.at[d], recv_s.at[d ^ 1], d).start()

    def sent_early(g, carry):
        for u in range(2):
            for d in DIRS:
                i = g * 2 + u
                row = table_ref[slots + d, i]
                first_ref[d, i] = block_row([(early_ref, 0)], now_ref, table_ref, row)
        return carry

    lax.fori_loop(0, sends // 2, sent_early, 0)

    for d in range(4):

        @pl.when(has[d])
        def _():
            remote(rows_out.at[d], rows_in.at[d], send_s.at[d], recv_s.at[d], d).wait_recv()

        @pl.when(jnp.logical_not(has[d]))
        def _():
            rows_in[d] = jnp.zeros(rows_in.shape[1:], F32)

    taken = jnp.concatenate(
        [rows_in[d] for d in range(4)] + [jnp.zeros((block - 32, block), F32)], axis=0
    )
    scales = taken.T
    for d in (0, 1, 2, 3):

        @pl.when(has[d])
        def _():
            remote(stage_a.at[d], halo_a.at[d], send_a.at[d], recv_a.at[d], d).wait_recv()

        @pl.when(jnp.logical_not(has[d]))
        def _():
            halo_a[d] = jnp.zeros(halo_a.shape[1:], BF16)

        for s in range(sends):
            scale = jnp.broadcast_to(scales[:, d * 8 + s : d * 8 + s + 1], (block, topics))
            now_ref[blocks + d * sends + s] = (scale * halo_a[d, s].astype(F32)).astype(BF16)

    def next_scaled(r, product):
        scale = doubled(scale_ref[r])
        current = ALPHA * scale * product + SEED * count_ref[r].astype(F32)
        return (scale * current).astype(BF16)

    def halo_copy(d, s):
        block_at = blocks + (d ^ 1) * sends + s
        return remote(
            stage_b.at[d, s], next_ref.at[block_at], send_b.at[d, s], recv_b.at[d ^ 1, s], d
        )

    def halo_arrival(d, s):
        block_at = blocks + d * sends + s
        return remote(
            stage_b.at[d, s], next_ref.at[block_at], send_b.at[d, s], recv_b.at[d, s], d
        )

    for s in range(sends):
        for d in DIRS:
            row = table_ref[slots + d, s]
            late = block_row([(late_ref, EARLY)], now_ref, table_ref, row)
            stage_b[d, s] = next_scaled(row, first_ref[d, s] + late)
        for d in DIRS:

            @pl.when(has[d])
            def _():
                halo_copy(d, s).start()

    def first_rows(g, carry):
        for u in range(WIDE):
            r = g * WIDE + u
            parts = [(early_ref, 0), (late_ref, EARLY)]
            scaled = next_scaled(r, block_row(parts, now_ref, table_ref, r))
            mine_ref[r] = scaled
            next_ref[r] = scaled
        return carry

    lax.fori_loop(0, blocks // WIDE, first_rows, 0)

    def second_early(g, carry):
        for u in range(WIDE):
            r = g * WIDE + u
            product = block_row([(early_ref, 0)], mine_ref, table_ref, r)
            scale = doubled(scale_ref[r])
            partial_ref[r] = ALPHA * scale * product + SEED * count_ref[r].astype(F32)
        return carry

    lax.fori_loop(0, blocks // WIDE, second_early, 0)

    for d in range(4):

        @pl.when(has[d])
        def _():
            for s in range(sends):
                halo_arrival(d, s).wait_recv()

        @pl.when(jnp.logical_not(has[d]))
        def _():
            for s in range(sends):
                next_ref[blocks + d * sends + s] = jnp.zeros((block, topics), BF16)

    for d in range(4):

        @pl.when(has[d])
        def _():
            remote(stage_a.at[d], halo_a.at[d], send_a.at[d], recv_a.at[d], d).wait_send()
            remote(rows_out.at[d], rows_in.at[d], send_s.at[d], recv_s.at[d], d).wait_send()
            for s in range(sends):
                halo_arrival(d, s).wait_send()


def finish_kernel(
    whole_ref, late_ref, next_ref, partial_ref, scale_ref, out_hbm, table_ref, out_ref, sem, sems
):
    blocks = out_ref.shape[0]
    table_copy = pltpu.make_async_copy(whole_ref.at[0:16, 0:128], table_ref, sem)
    table_copy.start()
    table_copy.wait()

    def write(g):
        rows = pl.ds(g * GROUP, GROUP)
        return pltpu.make_async_copy(out_ref.at[rows], out_hbm.at[rows], sems.at[g])

    def finish_rows(t, carry):
        for q in range(WIDE // GROUP):
            g = t * (WIDE // GROUP) + q
            for u in range(GROUP):
                r = g * GROUP + u
                product = block_row([(late_ref, EARLY)], next_ref, table_ref, r)
                out_ref[r] = partial_ref[r] + ALPHA * doubled(scale_ref[r]) * product
            write(g).start()
        return carry

    lax.fori_loop(0, blocks // WIDE, finish_rows, 0)
    for g in range(blocks // GROUP):
        write(g).wait()


def placed(rows, first, height, width):
    return jnp.pad(rows, ((first, height - first - rows.shape[0]), (0, width - rows.shape[1])))


def local(sizes, labels, weights, column_index, send_index, seed_doc, seed_topic):
    blocks, slots, block, _ = weights.shape
    topics = labels.shape[1]
    dirs, sends = send_index.shape[1:]
    halo = dirs * sends
    chunks = blocks // CHUNK
    seeds = seed_doc.shape[0]
    put = functools.partial(placed, height=24, width=seeds)
    table = put(column_index.T, 0) + put(send_index.reshape(dirs, sends), slots)
    table += put(seed_doc.reshape(1, seeds), 16) + put(seed_topic.reshape(1, seeds), 17)
    late, following, partial, scale = pl.pallas_call(
        functools.partial(spread_kernel, sizes),
        out_shape=(
            jax.ShapeDtypeStruct((blocks, slots - EARLY, block, block), BF16),
            jax.ShapeDtypeStruct((blocks + halo, block, topics), BF16),
            jax.ShapeDtypeStruct((blocks, block, topics), F32),
            jax.ShapeDtypeStruct((blocks, block, block), F32),
        ),
        in_specs=[VMEM, HBM, HBM],
        out_specs=(VMEM, VMEM, VMEM, VMEM),
        scratch_shapes=[
            pltpu.SMEM((16, 128), jnp.int32),
            pltpu.VMEM((blocks, EARLY, block, block), BF16),
            pltpu.VMEM((blocks, block, topics), F32),
            pltpu.VMEM((blocks + halo, block, topics), BF16),
            pltpu.VMEM((dirs, sends, block, topics), F32),
            pltpu.VMEM((blocks, block, topics), BF16),
            pltpu.VMEM((seed_doc.shape[0], topics), BF16),
            pltpu.VMEM((dirs, sends, block, topics), BF16),
            pltpu.VMEM((dirs, sends, block, topics), BF16),
            pltpu.VMEM((dirs, sends, block, topics), BF16),
            pltpu.VMEM((blocks, block, topics), BF16),
            pltpu.VMEM((dirs, 8, block), F32),
            pltpu.VMEM((dirs, 8, block), F32),
            pltpu.SemaphoreType.DMA,
            pltpu.SemaphoreType.DMA,
            pltpu.SemaphoreType.DMA((chunks,)),
            pltpu.SemaphoreType.DMA((chunks,)),
            pltpu.SemaphoreType.DMA((dirs,)),
            pltpu.SemaphoreType.DMA((dirs,)),
            pltpu.SemaphoreType.DMA((dirs, sends)),
            pltpu.SemaphoreType.DMA((dirs, sends)),
            pltpu.SemaphoreType.DMA((dirs,)),
            pltpu.SemaphoreType.DMA((dirs,)),
        ],
        compiler_params=pltpu.CompilerParams(
            collective_id=0, has_side_effects=True, vmem_limit_bytes=38 << 20
        ),
        name="spread",
    )(
        table,
        labels.reshape(blocks, block, topics),
        weights,
    )
    out = pl.pallas_call(
        finish_kernel,
        out_shape=jax.ShapeDtypeStruct((blocks, block, topics), F32),
        in_specs=[VMEM, VMEM, VMEM, VMEM, VMEM],
        out_specs=HBM,
        scratch_shapes=[
            pltpu.SMEM((16, 128), jnp.int32),
            pltpu.VMEM((blocks, block, topics), F32),
            pltpu.SemaphoreType.DMA,
            pltpu.SemaphoreType.DMA((blocks // GROUP,)),
        ],
        compiler_params=pltpu.CompilerParams(vmem_limit_bytes=30 << 20),
        name="finish",
    )(table, late, following, partial, scale)
    return out.reshape(blocks * block, topics)


def solution(mesh):
    sizes = (mesh.shape["gx"], mesh.shape["gy"])
    parts = P(("gx", "gy"))
    return jax.shard_map(
        functools.partial(local, sizes),
        mesh=mesh,
        in_specs=(parts,) * 6,
        out_specs=parts,
        check_vma=False,
    )
```

time: 27.8 us -> 25.3 us (0.910)
  the two profiles are of different devices: /device:TPU:104 before, /device:TPU:1 now
where the time goes in v2:
time: 25.3 us; the launch traced here: 25.1 us
  Pallas kernels  24.4 us (96%)
  other arithmetic  0.75 us (3%)
    pallas_call x1, Pallas kernels, local(): pl.pallas_call(functools.partial(spread_kernel, sizes), out_shape=(jax.Sh...  20.9 us
    pallas_call x1, Pallas kernels, local(): pl.pallas_call(finish_kernel, out_shape=jax.ShapeDtypeStruct((blocks, blo...  3.43 us
    add x1, other arithmetic, local(): table += put(seed_doc.reshape(1, seeds), 16) + put(seed_topic.reshape(1,...  0.75 us

profile of v2, /device:TPU:1, one launch (start us, length us, event | category | flops | bytes accessed | tf_op | source)
XLA Modules:
  0.0 25.1 jit_solution(16601667767464015198)
XLA Ops:
  0.0 0.8 %add_add_fusion.whole_ref = s32[24,256]{1,0:T(8,128)S(1)} fusion(s32[1,256]{1,0:T(1,128)} %bitcast.9, s32[1,256]{1,0:T(1,128)} %bitcast.10, s32[4,4]{1,0:T(4,128)} %bitcast.8, s32[12,32]{1,0:T(8,128)} %bitcast.7), kind=kLoop, calls=%fused_computation | loop fusion | flops 18432 | bytes 28224 | tf_op jit(solution)/shard_map/add | solution.py:344
  0.8 20.9 %spread.1 = (bf16[32,4,128,128]{3,2,1,0:T(8,128)(2,1)S(1)}, bf16[48,128,256]{2,1,0:T(8,128)(2,1)S(1)}, f32[32,128,256]{2,1,0:T(8,128)S(1)}, f32[32,128,128]{2,1,0:T(8,128)S(1)}) custom-call(s32[24,256]{1,0:T(8,128)S(1)} %add_add_fusion.whole_ref, f32[32,128,256]{2,1,0:T(8,128)} %bitcast.6, bf16[32,12,128,128]{3,2,1,0:T(8,128)(2,1)} %weights_hbm.1), custom_call_target="tpu_custom_call" | custom-call | tf_op jit(solution)/shard_map/spread/pallas_call | solution.py:345
  21.7 3.4 %finish.1 = f32[32,128,256]{2,1,0:T(8,128)} custom-call(s32[24,256]{1,0:T(8,128)S(1)} %add_add_fusion.whole_ref, bf16[32,4,128,128]{3,2,1,0:T(8,128)(2,1)S(1)} %get-tuple-element.9.late_ref, bf16[48,128,256]{2,1,0:T(8,128)(2,1)S(1)} %get-tuple-element.10.next_ref, f32[32,128,256]{2,1,0:T(8,128)S(1)} %get-tuple-element.11.partial_ref, ...), custom_call_target="tpu_custom_call" | custom-call | tf_op jit(solution)/shard_map/finish/pallas_call | solution.py:389

commit v3 on v2

--- a/solution.py
+++ b/solution.py
@@ -19,7 +19,7 @@
 
 EARLY = 8
 CHUNK = 4
-FIRST = 1
+FILLED = 16
 WIDE = 16
 GROUP = 4
 DIRS = (2, 3, 0, 1)
@@ -56,6 +56,7 @@
     labels_ref,
     now_ref,
     first_ref,
+    fill_ref,
     count_ref,
     hot_ref,
     stage_a,
@@ -118,9 +119,9 @@
     label_copy.start()
     table_copy = pltpu.make_async_copy(whole_ref.at[0:16, 0:128], table_ref, table_sem)
     table_copy.start()
-    for c in range(FIRST):
-        early_copy(c).start()
-        late_copy(c).start()
+    for c in range(chunks):
+        early_copy(c).start(priority=1)
+        late_copy(c).start(priority=1)
 
     barrier = pltpu.get_barrier_semaphore()
     for d in range(4):
@@ -133,9 +134,6 @@
 
     table_copy.wait()
     label_copy.wait()
-    for c in range(FIRST, chunks):
-        early_copy(c).start()
-        late_copy(c).start()
     for d in DIRS:
         for s in range(sends):
             stage_a[d, s] = labels_ref[table_ref[slots + d, s]].astype(BF16)
@@ -202,6 +200,14 @@
 
     lax.fori_loop(0, sends // 2, sent_early, 0)
 
+    def fill_rows(g, carry):
+        for u in range(WIDE):
+            r = g * WIDE + u
+            fill_ref[r] = block_row([(early_ref, 0)], now_ref, table_ref, r)
+        return carry
+
+    lax.fori_loop(0, FILLED // WIDE, fill_rows, 0)
+
     for d in range(4):
 
         @pl.when(has[d])
@@ -258,16 +264,27 @@
             def _():
                 halo_copy(d, s).start()
 
+    def keep(r, product):
+        scaled = next_scaled(r, product)
+        mine_ref[r] = scaled
+        next_ref[r] = scaled
+
+    def filled_rows(g, carry):
+        for u in range(WIDE):
+            r = g * WIDE + u
+            keep(r, fill_ref[r] + block_row([(late_ref, EARLY)], now_ref, table_ref, r))
+        return carry
+
+    lax.fori_loop(0, FILLED // WIDE, filled_rows, 0)
+
     def first_rows(g, carry):
         for u in range(WIDE):
             r = g * WIDE + u
             parts = [(early_ref, 0), (late_ref, EARLY)]
-            scaled = next_scaled(r, block_row(parts, now_ref, table_ref, r))
-            mine_ref[r] = scaled
-            next_ref[r] = scaled
-        return carry
-
-    lax.fori_loop(0, blocks // WIDE, first_rows, 0)
+            keep(r, block_row(parts, now_ref, table_ref, r))
+        return carry
+
+    lax.fori_loop(FILLED // WIDE, blocks // WIDE, first_rows, 0)
 
     def second_early(g, carry):
         for u in range(WIDE):
@@ -358,6 +375,7 @@
             pltpu.VMEM((blocks, block, topics), F32),
             pltpu.VMEM((blocks + halo, block, topics), BF16),
             pltpu.VMEM((dirs, sends, block, topics), F32),
+            pltpu.VMEM((FILLED, block, topics), F32),
             pltpu.VMEM((blocks, block, topics), BF16),
             pltpu.VMEM((seed_doc.shape[0], topics), BF16),
             pltpu.VMEM((dirs, sends, block, topics), BF16),

time: 25.3 us -> 24.5 us (0.968)
  the two profiles are of different devices: /device:TPU:1 before, /device:TPU:104 now
where the time goes in v3:
time: 24.5 us; the launch traced here: 24.1 us
  Pallas kernels  23.3 us (95%)
  other arithmetic  0.75 us (3%)
    pallas_call x1, Pallas kernels, local(): pl.pallas_call(functools.partial(spread_kernel, sizes), out_shape=(jax.Sh...  19.9 us
    pallas_call x1, Pallas kernels, local(): pl.pallas_call(finish_kernel, out_shape=jax.ShapeDtypeStruct((blocks, blo...  3.43 us
    add x1, other arithmetic, local(): table += put(seed_doc.reshape(1, seeds), 16) + put(seed_topic.reshape(1,...  0.75 us

profile of v3, /device:TPU:104, one launch (start us, length us, event | category | flops | bytes accessed | tf_op | source)
XLA Modules:
  0.0 24.1 jit_solution(12097890754171796103)
XLA Ops:
  0.0 0.8 %add_add_fusion.whole_ref = s32[24,256]{1,0:T(8,128)S(1)} fusion(s32[1,256]{1,0:T(1,128)} %bitcast.9, s32[1,256]{1,0:T(1,128)} %bitcast.10, s32[4,4]{1,0:T(4,128)} %bitcast.8, s32[12,32]{1,0:T(8,128)} %bitcast.7), kind=kLoop, calls=%fused_computation | loop fusion | flops 18432 | bytes 28224 | tf_op jit(solution)/shard_map/add | solution.py:361
  0.8 19.9 %spread.1 = (bf16[32,4,128,128]{3,2,1,0:T(8,128)(2,1)S(1)}, bf16[48,128,256]{2,1,0:T(8,128)(2,1)S(1)}, f32[32,128,256]{2,1,0:T(8,128)S(1)}, f32[32,128,128]{2,1,0:T(8,128)S(1)}) custom-call(s32[24,256]{1,0:T(8,128)S(1)} %add_add_fusion.whole_ref, f32[32,128,256]{2,1,0:T(8,128)} %bitcast.6, bf16[32,12,128,128]{3,2,1,0:T(8,128)(2,1)} %weights_hbm.1), custom_call_target="tpu_custom_call" | custom-call | tf_op jit(solution)/shard_map/spread/pallas_call | solution.py:362
  20.7 3.4 %finish.1 = f32[32,128,256]{2,1,0:T(8,128)} custom-call(s32[24,256]{1,0:T(8,128)S(1)} %add_add_fusion.whole_ref, bf16[32,4,128,128]{3,2,1,0:T(8,128)(2,1)S(1)} %get-tuple-element.9.late_ref, bf16[48,128,256]{2,1,0:T(8,128)(2,1)S(1)} %get-tuple-element.10.next_ref, f32[32,128,256]{2,1,0:T(8,128)S(1)} %get-tuple-element.11.partial_ref, ...), custom_call_target="tpu_custom_call" | custom-call | tf_op jit(solution)/shard_map/finish/pallas_call | solution.py:407

commit v4 on v3

--- a/solution.py
+++ b/solution.py
@@ -15,6 +15,7 @@
 BF16 = jnp.bfloat16
 F32 = jnp.float32
 VMEM = pl.BlockSpec(memory_space=pltpu.VMEM)
+SMEM = pl.BlockSpec(memory_space=pltpu.SMEM)
 HBM = pl.BlockSpec(memory_space=pl.ANY)
 
 EARLY = 8
@@ -44,14 +45,21 @@
 
 def spread_kernel(
     sizes,
-    whole_ref,
+    columns_hbm,
+    lists_hbm,
+    docs_hbm,
+    topics_hbm,
     labels_hbm,
     weights_hbm,
     late_ref,
     next_ref,
     partial_ref,
     scale_ref,
+    columns_ref,
     table_ref,
+    list_ref,
+    doc_ref,
+    topic_ref,
     early_ref,
     labels_ref,
     now_ref,
@@ -78,9 +86,8 @@
 ):
     outer, inner = sizes
     blocks, block, topics = labels_hbm.shape
-    seeds = whole_ref.shape[1]
+    seeds = docs_hbm.shape[1]
     sends = halo_a.shape[1]
-    slots = weights_hbm.shape[1]
     a, b = lax.axis_index("gx"), lax.axis_index("gy")
     has = [b > 0, b < inner - 1, a > 0, a < outer - 1]
     peer = [
@@ -117,8 +124,15 @@
         )
 
     label_copy.start()
-    table_copy = pltpu.make_async_copy(whole_ref.at[0:16, 0:128], table_ref, table_sem)
-    table_copy.start()
+    small = [
+        pltpu.make_async_copy(lists_hbm, list_ref, table_sem.at[0]),
+        pltpu.make_async_copy(columns_hbm, table_ref, table_sem.at[1]),
+        pltpu.make_async_copy(docs_hbm, doc_ref, table_sem.at[2]),
+        pltpu.make_async_copy(topics_hbm, topic_ref, table_sem.at[3]),
+        pltpu.make_async_copy(columns_hbm, columns_ref, table_sem.at[4]),
+    ]
+    for copy in small:
+        copy.start()
     for c in range(chunks):
         early_copy(c).start(priority=1)
         late_copy(c).start(priority=1)
@@ -132,21 +146,22 @@
 
     pl.semaphore_wait(barrier, sum(jnp.where(h, 1, 0) for h in has))
 
-    table_copy.wait()
+    for copy in small:
+        copy.wait()
     label_copy.wait()
     for d in DIRS:
         for s in range(sends):
-            stage_a[d, s] = labels_ref[table_ref[slots + d, s]].astype(BF16)
+            stage_a[d, s] = labels_ref[list_ref[d, s]].astype(BF16)
 
         @pl.when(has[d])
         def _():
             remote(stage_a.at[d], halo_a.at[d ^ 1], send_a.at[d], recv_a.at[d ^ 1], d).start()
 
-    wanted = jnp.broadcast_to(whole_ref[17:18], (topics, seeds))
+    wanted = jnp.broadcast_to(topic_ref[...], (topics, seeds))
     ours = lax.broadcasted_iota(jnp.int32, (topics, seeds), 0)
     hot_ref[...] = jnp.where(wanted == ours, 1.0, 0.0).astype(F32).T.astype(BF16)
 
-    wanted_docs = jnp.broadcast_to(whole_ref[16:17], (block, seeds))
+    wanted_docs = jnp.broadcast_to(doc_ref[...], (block, seeds))
 
     def count_rows(g, carry):
         for u in range(CHUNK):
@@ -181,7 +196,7 @@
     columns = jnp.zeros((block, block), F32)
     for d in range(4):
         for s in range(sends):
-            columns = jnp.where(lanes == d * 8 + s, scale_ref[table_ref[slots + d, s]], columns)
+            columns = jnp.where(lanes == d * 8 + s, scale_ref[list_ref[d, s]], columns)
     rows = columns.T
     for d in DIRS:
         rows_out[d] = rows[d * 8 : d * 8 + 8]
@@ -194,7 +209,7 @@
         for u in range(2):
             for d in DIRS:
                 i = g * 2 + u
-                row = table_ref[slots + d, i]
+                row = list_ref[d, i]
                 first_ref[d, i] = block_row([(early_ref, 0)], now_ref, table_ref, row)
         return carry
 
@@ -255,7 +270,7 @@
 
     for s in range(sends):
         for d in DIRS:
-            row = table_ref[slots + d, s]
+            row = list_ref[d, s]
             late = block_row([(late_ref, EARLY)], now_ref, table_ref, row)
             stage_b[d, s] = next_scaled(row, first_ref[d, s] + late)
         for d in DIRS:
@@ -319,12 +334,9 @@
 
 
 def finish_kernel(
-    whole_ref, late_ref, next_ref, partial_ref, scale_ref, out_hbm, table_ref, out_ref, sem, sems
+    table_ref, late_ref, next_ref, partial_ref, scale_ref, out_hbm, out_ref, sems
 ):
     blocks = out_ref.shape[0]
-    table_copy = pltpu.make_async_copy(whole_ref.at[0:16, 0:128], table_ref, sem)
-    table_copy.start()
-    table_copy.wait()
 
     def write(g):
         rows = pl.ds(g * GROUP, GROUP)
@@ -345,8 +357,8 @@
         write(g).wait()
 
 
-def placed(rows, first, height, width):
-    return jnp.pad(rows, ((first, height - first - rows.shape[0]), (0, width - rows.shape[1])))
+def in_place(array):
+    return pltpu.with_memory_space_constraint(array, pltpu.HBM)
 
 
 def local(sizes, labels, weights, column_index, send_index, seed_doc, seed_topic):
@@ -356,21 +368,22 @@
     halo = dirs * sends
     chunks = blocks // CHUNK
     seeds = seed_doc.shape[0]
-    put = functools.partial(placed, height=24, width=seeds)
-    table = put(column_index.T, 0) + put(send_index.reshape(dirs, sends), slots)
-    table += put(seed_doc.reshape(1, seeds), 16) + put(seed_topic.reshape(1, seeds), 17)
-    late, following, partial, scale = pl.pallas_call(
+    late, following, partial, scale, columns = pl.pallas_call(
         functools.partial(spread_kernel, sizes),
         out_shape=(
             jax.ShapeDtypeStruct((blocks, slots - EARLY, block, block), BF16),
             jax.ShapeDtypeStruct((blocks + halo, block, topics), BF16),
             jax.ShapeDtypeStruct((blocks, block, topics), F32),
             jax.ShapeDtypeStruct((blocks, block, block), F32),
+            jax.ShapeDtypeStruct((slots, blocks), jnp.int32),
         ),
-        in_specs=[VMEM, HBM, HBM],
-        out_specs=(VMEM, VMEM, VMEM, VMEM),
+        in_specs=[HBM] * 6,
+        out_specs=(VMEM,) * 5,
         scratch_shapes=[
-            pltpu.SMEM((16, 128), jnp.int32),
+            pltpu.SMEM((slots, blocks), jnp.int32),
+            pltpu.SMEM((dirs, sends), jnp.int32),
+            pltpu.VMEM((1, seeds), jnp.int32),
+            pltpu.VMEM((1, seeds), jnp.int32),
             pltpu.VMEM((blocks, EARLY, block, block), BF16),
             pltpu.VMEM((blocks, block, topics), F32),
             pltpu.VMEM((blocks + halo, block, topics), BF16),
@@ -384,7 +397,7 @@
             pltpu.VMEM((blocks, block, topics), BF16),
             pltpu.VMEM((dirs, 8, block), F32),
             pltpu.VMEM((dirs, 8, block), F32),
-            pltpu.SemaphoreType.DMA,
+            pltpu.SemaphoreType.DMA((5,)),
             pltpu.SemaphoreType.DMA,
             pltpu.SemaphoreType.DMA((chunks,)),
             pltpu.SemaphoreType.DMA((chunks,)),
@@ -400,24 +413,25 @@
         ),
         name="spread",
     )(
-        table,
+        in_place(column_index.T),
+        in_place(send_index.reshape(dirs, sends)),
+        in_place(seed_doc.reshape(1, seeds)),
+        in_place(seed_topic.reshape(1, seeds)),
         labels.reshape(blocks, block, topics),
         weights,
     )
     out = pl.pallas_call(
         finish_kernel,
         out_shape=jax.ShapeDtypeStruct((blocks, block, topics), F32),
-        in_specs=[VMEM, VMEM, VMEM, VMEM, VMEM],
+        in_specs=[SMEM, VMEM, VMEM, VMEM, VMEM],
         out_specs=HBM,
         scratch_shapes=[
-            pltpu.SMEM((16, 128), jnp.int32),
             pltpu.VMEM((blocks, block, topics), F32),
-            pltpu.SemaphoreType.DMA,
             pltpu.SemaphoreType.DMA((blocks // GROUP,)),
         ],
         compiler_params=pltpu.CompilerParams(vmem_limit_bytes=30 << 20),
         name="finish",
-    )(table, late, following, partial, scale)
+    )(columns, late, following, partial, scale)
     return out.reshape(blocks * block, topics)
 
 

time: 24.5 us -> 24.2 us (0.988)
  other arithmetic: 0.75 us -> 0 us
  Pallas kernels: 23.3 us -> 23.8 us
    add x1 -> x0, other arithmetic: 0.75 us -> none  [local(): table += put(seed_doc.reshape(1, seeds), 16) + put(seed_topic.reshape(1,...]
    pallas_call x1, Pallas kernels: 19.9 us -> 20.3 us  [local(): pl.pallas_call(functools.partial(spread_kernel, sizes), out_shape=(jax.Sh...]
where the time goes in v4:
time: 24.2 us; the launch traced here: 23.8 us
  Pallas kernels  23.8 us (98%)
    pallas_call x1, Pallas kernels, local(): pl.pallas_call(functools.partial(spread_kernel, sizes), out_shape=(jax.Sh...  20.3 us
    pallas_call x1, Pallas kernels, local(): pl.pallas_call(finish_kernel, out_shape=jax.ShapeDtypeStruct((blocks, blo...  3.54 us

profile of v4, /device:TPU:104, one launch (start us, length us, event | category | flops | bytes accessed | tf_op | source)
XLA Modules:
  0.0 23.8 jit_solution(2848972889740925628)
XLA Ops:
  0.0 20.3 %spread.1 = (bf16[32,4,128,128]{3,2,1,0:T(8,128)(2,1)S(1)}, bf16[48,128,256]{2,1,0:T(8,128)(2,1)S(1)}, f32[32,128,256]{2,1,0:T(8,128)S(1)}, f32[32,128,128]{2,1,0:T(8,128)S(1)}, s32[12,32]{1,0:T(8,128)S(1)}) custom-call(s32[12,32]{1,0:T(8,128)} %bitcast.7, s32[4,4]{1,0:T(4,128)} %bitcast.8, s32[1,256]{1,0:T(1,128)} %bitcast.9, s32[1,256]{1,0:T(1,128)} %bitcast.10, ...), custom_call_target="tpu_custom_call" | custom-call | tf_op jit(solution)/shard_map/spread/pallas_call | solution.py:371
  20.3 3.5 %finish.1 = f32[32,128,256]{2,1,0:T(8,128)} custom-call(s32[12,32]{1,0:T(8,128)S(1)} %get-tuple-element.10.table_ref, bf16[32,4,128,128]{3,2,1,0:T(8,128)(2,1)S(1)} %get-tuple-element.11.late_ref, bf16[48,128,256]{2,1,0:T(8,128)(2,1)S(1)} %get-tuple-element.12.next_ref, f32[32,128,256]{2,1,0:T(8,128)S(1)} %get-tuple-element.13.partial_ref, ...), custom_call_target="tpu_custom_call" | custom-call | tf_op jit(solution)/shard_map/finish/pallas_call | solution.py:423
